TPU v7x, 128 devices: a whole 4x4x4 slice. The times are simulated.
128 devices in a mesh: out: 8 (over x, y_hi), blk: 16 (over y_lo, z, core).
Axes of the slice: x: 4, y: 4 (y_hi: 2, y_lo: 2; y = y_hi * 2 + y_lo), z: 4, core: 2. Of those that a mesh axis runs over, the one named last changes fastest.
Arguments:
- checkpoints: bfloat16 [8, 5, 128, 2048], P('out', None, None, 'blk'), may hold values from -4 to 4
- owner: int32 [8], replicated, may hold values from 0 to 7, each once
- flux_matrix: float32 [5, 5], replicated, may hold values from -2.5 to 2.5
- row_link: int32 [16, 128], P('blk'), may hold values from 0 to 127, each once within a row
- blade_group: int32 [96], replicated, may hold values from 0 to 15
- forcing: float32 [5, 128, 2048], P(None, None, 'blk'), may hold values from -6 to 6
Outputs:
- adjoint: float32 [16, 4, 5, 128, 2048], P('out', None, None, None, 'blk')
- sensitivity: float32 [16, 4], P('out')
Inputs may be any that keep to these rules, and one draw needn't show every extreme that they name: Each tile's row_link is a permutation of its rows.
All inputs are finite; a program needn't handle non-finite values.
Results may differ from a plain program's by a relative error of at most 0.0003.
Values may be sent and summed in bfloat16 or wider, within the bound.
A program may use at most 128 MiB of HBM per device.

v0:
```python
import math

import jax
import jax.numpy as jnp
from jax import lax
from jax.sharding import PartitionSpec as P

FIELDS = 5
BLADES = 96
AMP = 4
GRP_DEV = 2
STEPS = 3


time_step = 0.25
second_diff = 0.1
fourth_diff = 0.02
link_weight = 0.5
two_pi = 2.0 * math.pi


def broadcast(block, axis, holder):
    block = jnp.where(lax.axis_index(axis) == holder, block, jnp.zeros_like(block))
    return lax.psum(block, axis)


def padded_2(shard, sides, width):
    for axis, dim in sides:
        devices, length = (lax.axis_size(axis), shard.shape[dim])
        up = [(i, (i + 1) % devices) for i in range(devices)]
        down = [(j, i) for i, j in up]
        last = lax.slice_in_dim(shard, length - width, length, axis=dim)
        leading = lax.slice_in_dim(shard, 0, width, axis=dim)
        before = lax.ppermute(last, axis, up)
        after = lax.ppermute(leading, axis, down)
        shard = jnp.concatenate([before, shard, after], axis=dim)
    return shard


def source_for(columns, total, blade_group, group_ids):
    scaled = columns * BLADES
    blade_of = scaled // total
    phase = (scaled % total).astype(jnp.float32) / total
    onehot = (blade_of[:, None] == jnp.arange(BLADES, dtype=jnp.int32)[None, :]).astype(jnp.int32)
    group_of = jnp.sum(onehot * blade_group[None, :], axis=1)
    member = (group_of[None, :] == group_ids[:, None]).astype(jnp.float32)
    amp_index = jnp.arange(AMP, dtype=jnp.int32)
    order = (amp_index // 2 + 1).astype(jnp.float32)
    angle = two_pi * order[:, None] * phase[None, :]
    harmonic = jnp.where((amp_index % 2 == 0)[:, None], jnp.cos(angle), jnp.sin(angle))
    return member[:, None, :] * harmonic[None, :, :]


def update(center, state, flux_matrix, linked):
    inner_mu = center[..., 2:-2]
    plus_one = center[..., 3:-1]
    minus_one = center[..., 1:-3]
    plus_two = center[..., 4:]
    minus_two = center[..., :-4]
    is_velocity = (jnp.arange(FIELDS) == 1).astype(jnp.float32)[None, None, :, None, None]
    diff = (minus_one - plus_one) * 0.5
    flux_part = jnp.einsum("fe,gafrc->gaerc", flux_matrix, diff, precision=lax.Precision.HIGHEST)
    inner = jnp.sum(state[None, None] * diff, axis=2, keepdims=True)
    jac = flux_part + 0.5 * state[1][None, None, None] * diff + 0.5 * is_velocity * inner
    lapl = plus_one - 2.0 * inner_mu + minus_one
    quart = plus_two - 4.0 * plus_one + 6.0 * inner_mu - 4.0 * minus_one + minus_two
    rows_part = inner_mu - linked
    return inner_mu - time_step * (
        jac - second_diff * lapl + fourth_diff * quart + link_weight * rows_part
    )


def on_device(checkpoints, owner, flux_matrix, row_link, blade_group, forcing):
    cycle = lax.axis_size("blk")
    width = forcing.shape[2]
    rows = forcing.shape[1]
    total = width * cycle
    start = lax.axis_index("blk") * width
    column = start + jnp.arange(width, dtype=jnp.int32)
    group_ids = lax.axis_index("out") * GRP_DEV + jnp.arange(GRP_DEV, dtype=jnp.int32)
    weight_col = 1.0 + 2.0 * column.astype(jnp.float32) / total
    weighted = forcing * weight_col[None, None, :]
    norm_scale = 1.0 / math.sqrt(FIELDS * rows * total)
    states = [
        broadcast(checkpoints[0], "out", owner[step]).astype(jnp.float32) for step in range(STEPS)
    ]
    sens = jnp.zeros((GRP_DEV, AMP), jnp.float32)
    inverse = jnp.argsort(row_link[0])
    pattern = source_for(column, total, blade_group, group_ids)
    source_term = forcing[None, None] * pattern[:, :, None, None, :]
    adjoint = jnp.zeros(source_term.shape, jnp.float32)
    for step in reversed(range(STEPS)):
        center = adjoint + source_term
        padded = padded_2(center, (("blk", 4),), 2)
        linked = jnp.take(center, inverse, axis=3)
        adjoint = update(padded, states[step], flux_matrix, linked)
        sens = sens + jnp.sum(adjoint * weighted[None, None], axis=(2, 3, 4)) * norm_scale
    sens = lax.psum(sens, "blk")
    return (adjoint, sens)


def solution(mesh):
    return jax.shard_map(
        on_device,
        mesh=mesh,
        in_specs=(P("out", None, None, "blk"), P(), P(), P("blk", None), P(), P(None, None, "blk")),
        out_specs=(P("out", None, None, None, "blk"), P("out", None)),
        check_vma=False,
    )
```

profile of v0, /device:TPU:1, one launch (start us, length us, event | category | flops | bytes accessed | tf_op | source)
XLA Modules:
  0.0 328.6 jit_solution(1285741374218219164)
XLA Ops:
  7.3 1.2 copy.71
  8.5 0.8 select_reduce_fusion
  9.4 0.3 broadcast_multiply_fusion
  9.7 4.6 %fusion.105 = (f32[2,4,5,128,2]{4,2,3,1,0:T(8,128)}, f32[2,4,5,128,2]{4,2,3,1,0:T(8,128)}) fusion(f32[2,4,5,128,128]{4,2,3,1,0:T(8,128)S(1)} %broadcast_multiply_fusion), kind=kLoop, calls=%fused_computation.163 | loop fusion | bytes 163840 | tf_op jit(solution)/shard_map/slice | solution.py:33
  14.4 2.7 copy.72
  17.1 3.1 collective-permute-start
  20.2 2.6 copy.74
  22.9 0.6 fusion.106
  25.4 0.8 select_bitcast_fusion
  26.3 2.5 sort.17
  28.9 3.9 %copy.78 = f32[2,4,5,128,128]{4,1,3,2,0:T(4,128)S(1)} copy(f32[2,4,5,128,128]{4,2,3,1,0:T(8,128)} %copy-done.1) | data formatting | bytes 5242880 | tf_op jit(solution)/shard_map/mul | solution.py:90
  32.8 1.0 copy.96
  33.8 3.9 %gather_fusion = f32[128,2,4,5,128]{4,2,3,1,0:T(4,128)} fusion(f32[2,4,5,128,128]{4,1,3,2,0:T(4,128)S(1)} %copy.78, s32[1024]{0:T(1024)S(1)} %pad_clamp_fusion), kind=kCustom, calls=%fused_computation.clone | custom fusion | bytes 5243392 | tf_op jit(solution)/shard_map/jit(_take)/gather | solution.py:95
  37.7 2.8 copy.73
  40.6 2.6 copy.75
  43.2 65.9 %all-reduce.3.cloned.1.call-done = (bf16[5,128,128]{2,1,0:T(8,128)(2,1)}, bf16[5,128,128]{2,1,0:T(8,128)(2,1)}, bf16[5,128,128]{2,1,0:T(8,128)(2,1)}) async-done(((bf16[5,128,128]{2,1,0:T(8,128)(2,1)}, bf16[5,128,128]{2,1,0:T(8,128)(2,1)}, bf16[5,128,128]{2,1,0:T(8,128)(2,1)}), (bf16[5,128,128]{2,1,0:T(8,128)(2,1)}, bf16[5,128,128]{2,1,0:T(8,128)(2,1)}, ...) | async-done | bytes 491536 | tf_op jit(solution)/shard_map/psum | solution.py:24
  109.1 0.9 broadcast_multiply_fusion.4
  110.1 0.9 convert_element_type.45
  111.0 1.7 broadcast_multiply_fusion.3
  112.7 0.9 convert_element_type.46
  113.9 12.4 %fusion.2 = f32[2,4,5,128,128]{4,2,3,1,0:T(8,128)} fusion(f32[5,128,128]{2,0,1:T(8,128)S(1)} %copy.77, f32[2,4,5,128,2]{4,2,3,1,0:T(8,128)} %copy.73, f32[2,4,5,128,128]{4,2,3,1,0:T(8,128)} %copy-done.1, f32[2,4,5,128,2]{4,2,3,1,0:T(8,128)} %copy.75), kind=kOutput, calls=%fused_computation.5 | output fusion | flops 2752516 | bytes 5652480 | tf_op jit(solution)/shard_map/mul | solution.py:64
  126.3 21.4 %multiply_add_fusion.1 = (f32[2,4,5,128,128]{4,2,3,1,0:T(8,128)S(1)}, f32[2,4,5,128,128]{4,2,3,1,0:T(8,128)}) fusion(f32[2,4,128]{2,1,0:T(4,128)S(1)} %broadcast_multiply_fusion.5, f32[5,128,128]{2,0,1:T(8,128)S(1)} %copy.71, f32[128,2,4,5,128]{4,2,3,1,0:T(4,128)} %gather_fusion, pred[128]{0:T(512)(128)(4,1)S(1)} %compare_and_fusion, ...), kind=kOutput, calls=%fused_computation.7 | convolution fusion | flops 62259200 | bytes 37823488 | tf_op jit(solution)/shard_map/fe,gafrc->gaerc/dot_general | solution.py:62
  147.6 4.7 %fusion.104 = (f32[2,4,5,128,2]{4,2,3,1,0:T(8,128)}, f32[2,4,5,128,2]{4,2,3,1,0:T(8,128)}) fusion(f32[2,4,5,128,128]{4,2,3,1,0:T(8,128)S(1)} %get-tuple-element.31), kind=kLoop, calls=%fused_computation.162 | loop fusion | bytes 163840 | tf_op jit(solution)/shard_map/slice | solution.py:33
  152.3 3.3 copy.80
  155.6 6.9 %collective-permute-start.2 = (f32[2,4,5,128,2]{3,1,4,2,0:T(4,128)}, f32[2,4,5,128,2]{3,1,4,2,0:T(4,128)}, u32[]{:S(2)}, u32[]{:S(2)}) collective-permute-start(f32[2,4,5,128,2]{3,1,4,2,0:T(4,128)} %copy.80), channel_id=1, source_target_pairs={{0,1},{1,2},{2,3},{3,4},{4,5},{5,6},{6,7},{7,8},{8,9},{9,10},{10,1... | collective-permute-start | bytes 122888 | tf_op jit(solution)/shard_map/ppermute | solution.py:34
  162.5 3.2 copy.82
  165.8 3.9 %copy.86 = f32[2,4,5,128,128]{4,1,3,2,0:T(4,128)S(1)} copy(f32[2,4,5,128,128]{4,2,3,1,0:T(8,128)} %copy-done.5) | data formatting | bytes 5242880 | tf_op jit(solution)/shard_map/add | solution.py:93
  169.7 0.7 convert_element_type.47
  170.5 3.9 %gather_fusion.1 = f32[128,2,4,5,128]{4,2,3,1,0:T(4,128)} fusion(f32[2,4,5,128,128]{4,1,3,2,0:T(4,128)S(1)} %copy.86, s32[1024]{0:T(1024)S(1)} %pad_clamp_fusion), kind=kCustom, calls=%fused_computation.1.clone | custom fusion | bytes 5243392 | tf_op jit(solution)/shard_map/jit(_take)/gather | solution.py:95
  174.4 1.2 copy.85
  175.6 3.5 %copy.81 = f32[2,4,5,128,2]{4,2,3,1,0:T(8,128)} copy(f32[2,4,5,128,2]{3,1,4,2,0:T(4,128)} %collective-permute-done.2) | data formatting | bytes 81920 | tf_op jit(solution)/shard_map/ppermute | solution.py:34
  179.1 3.3 %copy.83 = f32[2,4,5,128,2]{4,2,3,1,0:T(8,128)} copy(f32[2,4,5,128,2]{3,1,4,2,0:T(4,128)} %collective-permute-done.3) | data formatting | bytes 81920 | tf_op jit(solution)/shard_map/ppermute | solution.py:35
  182.5 12.2 %fusion.1 = f32[2,4,5,128,128]{4,2,3,1,0:T(8,128)} fusion(f32[5,128,128]{2,0,1:T(8,128)S(1)} %copy.85, f32[2,4,5,128,2]{4,2,3,1,0:T(8,128)} %copy.81, f32[2,4,5,128,128]{4,2,3,1,0:T(8,128)} %copy-done.5, f32[2,4,5,128,2]{4,2,3,1,0:T(8,128)} %copy.83), kind=kOutput, calls=%fused_computation.4 | output fusion | flops 2752516 | bytes 5652480 | tf_op jit(solution)/shard_map/mul | solution.py:64
  194.7 26.9 %multiply_add_fusion = (f32[2,4,5,128,128]{4,2,3,1,0:T(8,128)S(1)}, f32[2,4,5,128,128]{4,2,3,1,0:T(8,128)}) fusion(f32[2,4,128]{2,1,0:T(4,128)S(1)} %broadcast_multiply_fusion.5, f32[5,128,128]{2,0,1:T(8,128)S(1)} %copy.71, f32[2,4,5,128,128]{4,2,3,1,0:T(8,128)} %copy-done.5, f32[128,2,4,5,128]{4,2,3,1,0:T(4,128)} %gather_fusion.1, ...), kind=kOutput, calls=%fused_computation.6 | convolution fusion | flops 62259200 | bytes 37622008 | tf_op jit(solution)/shard_map/fe,gafrc->gaerc/dot_general | solution.py:62
  221.5 4.7 %fusion.103 = (f32[2,4,5,128,2]{4,2,3,1,0:T(8,128)}, f32[2,4,5,128,2]{4,2,3,1,0:T(8,128)}) fusion(f32[2,4,5,128,128]{4,2,3,1,0:T(8,128)S(1)} %get-tuple-element.33), kind=kLoop, calls=%fused_computation.161 | loop fusion | bytes 163840 | tf_op jit(solution)/shard_map/slice | solution.py:33
  226.2 3.2 copy.88
  229.5 1.7 collective-permute-start.4
  231.2 3.2 copy.90
  234.4 0.9 collective-permute-start.5
  235.3 0.8 fusion.74
  236.4 3.9 %copy.94 = f32[2,4,5,128,128]{4,1,3,2,0:T(4,128)S(1)} copy(f32[2,4,5,128,128]{4,2,3,1,0:T(8,128)} %copy-done.3) | data formatting | bytes 5242880 | tf_op jit(solution)/shard_map/add | solution.py:93
  240.3 3.9 %gather_fusion.2 = f32[128,2,4,5,128]{4,2,3,1,0:T(4,128)} fusion(f32[2,4,5,128,128]{4,1,3,2,0:T(4,128)S(1)} %copy.94, s32[1024]{0:T(1024)S(1)} %pad_clamp_fusion), kind=kCustom, calls=%fused_computation.2.clone | custom fusion | bytes 5243392 | tf_op jit(solution)/shard_map/jit(_take)/gather | solution.py:95
  244.2 3.6 %copy.89 = f32[2,4,5,128,2]{4,2,3,1,0:T(8,128)} copy(f32[2,4,5,128,2]{3,1,4,2,0:T(4,128)} %collective-permute-done.4) | data formatting | bytes 81920 | tf_op jit(solution)/shard_map/ppermute | solution.py:34
  247.8 3.3 %copy.91 = f32[2,4,5,128,2]{4,2,3,1,0:T(8,128)} copy(f32[2,4,5,128,2]{3,1,4,2,0:T(4,128)} %collective-permute-done.5) | data formatting | bytes 81920 | tf_op jit(solution)/shard_map/ppermute | solution.py:35
  251.1 12.3 %fusion = f32[2,4,5,128,128]{4,2,3,1,0:T(8,128)} fusion(f32[5,128,128]{2,0,1:T(8,128)S(1)} %copy.93, f32[2,4,5,128,2]{4,2,3,1,0:T(8,128)} %copy.89, f32[2,4,5,128,128]{4,2,3,1,0:T(8,128)} %copy-done.3, f32[2,4,5,128,2]{4,2,3,1,0:T(8,128)} %copy.91), kind=kOutput, calls=%fused_computation.3 | output fusion | flops 2752516 | bytes 5652480 | tf_op jit(solution)/shard_map/mul | solution.py:64
  263.4 22.8 %multiply_reduce_fusion.1 = (f32[2,4]{1,0:T(2,128)S(1)}, f32[2,4]{1,0:T(2,128)S(1)}, f32[2,4]{1,0:T(2,128)S(1)}, f32[2,4,5,128,128]{4,2,3,1,0:T(8,128)}) fusion(f32[2,4,5,128,128]{4,2,3,1,0:T(8,128)} %get-tuple-element.34, f32[5,128,128]{2,0,1:T(8,128)} %copy.96, f32[2,4,5,128,128]{4,2,3,1,0:T(8,128)} %get-tuple-element.32, ...), kind=kOutput, calls=%fused_computation.83 | convolution fusion | flops 64880616 | bytes 43586656 | tf_op jit(solution)/shard_map/fe,gafrc->gaerc/dot_general | solution.py:62
  286.3 4.1 %copy.97 = f32[2,4,5,128,128]{4,3,2,1,0:T(8,128)} copy(f32[2,4,5,128,128]{4,2,3,1,0:T(8,128)} %get-tuple-element.35) | data formatting | bytes 5242880
  290.4 30.9 %psum.31 = f32[2,4]{1,0:T(2,128)} all-reduce(f32[2,4]{1,0:T(2,128)S(1)} %add_multiply_fusion), channel_id=1, replica_groups=mesh['out'=8,'blk'=16] {'blk'}, use_global_device_ids=true, to_apply=%region_11.13 | all-reduce | flops 8 | bytes 64 | tf_op jit(solution)/shard_map/psum | solution.py:98
  (60 shorter events, 0.9 us)
Async XLA Ops:
  7.2 119.1 %copy-start = (f32[5,5]{1,0:T(8,128)S(1)}, f32[5,5]{1,0:T(8,128)}, u32[]{:S(2)}) copy-start(f32[5,5]{1,0:T(8,128)} %param.10) | copy-start | bytes 304
  7.2 102.0 %all-reduce.3.cloned.1.call-start = ((), (), s32[]{:S(2)}) async-start(), calls=%async_computation | async-start | bytes 983040 | tf_op jit(solution)/shard_map/psum | solution.py:24
  9.7 4.7 %copy-start.1 = (f32[2,4,5,128,128]{4,2,3,1,0:T(8,128)}, f32[2,4,5,128,128]{4,2,3,1,0:T(8,128)S(1)}, u32[]{:S(2)}) copy-start(f32[2,4,5,128,128]{4,2,3,1,0:T(8,128)S(1)} %broadcast_multiply_fusion) | copy-start | bytes 7864324
  14.4 8.5 %copy-start.10 = (s32[8]{0:T(128)S(1)}, s32[8]{0:T(128)}, u32[]{:S(2)}) copy-start(s32[8]{0:T(128)} %param.9) | copy-start | bytes 100
  14.4 11.0 %copy-start.9 = (bf16[1,5,128,128]{3,2,1,0:T(8,128)(2,1)S(1)}, bf16[1,5,128,128]{3,2,1,0:T(8,128)(2,1)}, u32[]{:S(2)}) copy-start(bf16[1,5,128,128]{3,2,1,0:T(8,128)(2,1)} %param.8) | copy-start | bytes 491524
  14.4 11.9 %copy-start.11 = (s32[1,128]{1,0:T(1,128)S(1)}, s32[1,128]{1,0:T(1,128)}, u32[]{:S(2)}) copy-start(s32[1,128]{1,0:T(1,128)} %param.11) | copy-start | bytes 1540
  14.4 14.4 %copy-start.6 = (f32[5,128,128]{2,1,0:T(8,128)S(1)}, f32[5,128,128]{2,1,0:T(8,128)}, u32[]{:S(2)}) copy-start(f32[5,128,128]{2,1,0:T(8,128)} %param.13) | copy-start | bytes 983044
  17.1 20.7 %collective-permute-start = (f32[2,4,5,128,2]{3,1,4,2,0:T(4,128)S(1)}, f32[2,4,5,128,2]{3,1,4,2,0:T(4,128)S(1)}, u32[]{:S(2)}, u32[]{:S(2)}) collective-permute-start(f32[2,4,5,128,2]{3,1,4,2,0:T(4,128)S(1)} %copy.72), channel_id=1, source_target_pairs={{0,1},{1,2},{2,3},{3,4},{4,5},{5,6},{6,7},{7,8},{8,9},{9,10},{10,1... | collective-permute-start | bytes 122888 | tf_op jit(solution)/shard_map/ppermute | solution.py:34
  22.8 17.8 %collective-permute-start.1 = (f32[2,4,5,128,2]{3,1,4,2,0:T(4,128)S(1)}, f32[2,4,5,128,2]{3,1,4,2,0:T(4,128)S(1)}, u32[]{:S(2)}, u32[]{:S(2)}) collective-permute-start(f32[2,4,5,128,2]{3,1,4,2,0:T(4,128)S(1)} %copy.74), channel_id=1, source_target_pairs={{1,0},{2,1},{3,2},{4,3},{5,4},{6,5},{7,6},{8,7},{9,8},{10,9},{11,1... | collective-permute-start | bytes 122888 | tf_op jit(solution)/shard_map/ppermute | solution.py:35
  28.9 97.4 %copy-start.12 = (f32[5]{0:T(128)}, f32[5]{0:T(128)S(1)}, u32[]{:S(2)}) copy-start(f32[5]{0:T(128)S(1)} %compare_select_fusion.1) | copy-start | bytes 64
  113.9 12.4 %copy-start.2 = (f32[2,4,5,128,128]{4,2,3,1,0:T(8,128)S(1)}, f32[2,4,5,128,128]{4,2,3,1,0:T(8,128)}, u32[]{:S(2)}) copy-start(f32[2,4,5,128,128]{4,2,3,1,0:T(8,128)} %copy-done.1) | copy-start | bytes 7864324
  147.6 4.7 %copy-start.5 = (f32[2,4,5,128,128]{4,2,3,1,0:T(8,128)}, f32[2,4,5,128,128]{4,2,3,1,0:T(8,128)S(1)}, u32[]{:S(2)}) copy-start(f32[2,4,5,128,128]{4,2,3,1,0:T(8,128)S(1)} %get-tuple-element.31) | copy-start | bytes 7864324
  152.3 13.4 %copy-start.7 = (bf16[5,128,128]{2,1,0:T(8,128)(2,1)S(1)}, bf16[5,128,128]{2,1,0:T(8,128)(2,1)}, u32[]{:S(2)}) copy-start(bf16[5,128,128]{2,1,0:T(8,128)(2,1)} %get-tuple-element.18) | copy-start | bytes 491524
  155.6 20.0 %collective-permute-start.2 = (f32[2,4,5,128,2]{3,1,4,2,0:T(4,128)}, f32[2,4,5,128,2]{3,1,4,2,0:T(4,128)}, u32[]{:S(2)}, u32[]{:S(2)}) collective-permute-start(f32[2,4,5,128,2]{3,1,4,2,0:T(4,128)} %copy.80), channel_id=1, source_target_pairs={{0,1},{1,2},{2,3},{3,4},{4,5},{5,6},{6,7},{7,8},{8,9},{9,10},{10,1... | collective-permute-start | bytes 122888 | tf_op jit(solution)/shard_map/ppermute | solution.py:34
  165.7 4.0 %copy-start.8 = (bf16[5,128,128]{2,1,0:T(8,128)(2,1)S(1)}, bf16[5,128,128]{2,1,0:T(8,128)(2,1)}, u32[]{:S(2)}) copy-start(bf16[5,128,128]{2,1,0:T(8,128)(2,1)} %get-tuple-element.18) | copy-start | bytes 491524
  165.8 13.4 %collective-permute-start.3 = (f32[2,4,5,128,2]{3,1,4,2,0:T(4,128)}, f32[2,4,5,128,2]{3,1,4,2,0:T(4,128)}, u32[]{:S(2)}, u32[]{:S(2)}) collective-permute-start(f32[2,4,5,128,2]{3,1,4,2,0:T(4,128)} %copy.82), channel_id=1, source_target_pairs={{1,0},{2,1},{3,2},{4,3},{5,4},{6,5},{7,6},{8,7},{9,8},{10,9},{11,1... | collective-permute-start | bytes 122888 | tf_op jit(solution)/shard_map/ppermute | solution.py:35
  182.4 12.2 %copy-start.13 = (f32[5]{0:T(128)S(1)}, f32[5]{0:T(128)}, u32[]{:S(2)}) copy-start(f32[5]{0:T(128)} %copy-done.12) | copy-start | bytes 64
  221.5 4.7 %copy-start.3 = (f32[2,4,5,128,128]{4,2,3,1,0:T(8,128)}, f32[2,4,5,128,128]{4,2,3,1,0:T(8,128)S(1)}, u32[]{:S(2)}) copy-start(f32[2,4,5,128,128]{4,2,3,1,0:T(8,128)S(1)} %get-tuple-element.33) | copy-start | bytes 7864324
  229.5 14.7 %collective-permute-start.4 = (f32[2,4,5,128,2]{3,1,4,2,0:T(4,128)}, f32[2,4,5,128,2]{3,1,4,2,0:T(4,128)}, u32[]{:S(2)}, u32[]{:S(2)}) collective-permute-start(f32[2,4,5,128,2]{3,1,4,2,0:T(4,128)} %copy.88), channel_id=1, source_target_pairs={{0,1},{1,2},{2,3},{3,4},{4,5},{5,6},{6,7},{7,8},{8,9},{9,10},{10,1... | collective-permute-start | bytes 122888 | tf_op jit(solution)/shard_map/ppermute | solution.py:34
  234.4 13.4 %collective-permute-start.5 = (f32[2,4,5,128,2]{3,1,4,2,0:T(4,128)}, f32[2,4,5,128,2]{3,1,4,2,0:T(4,128)}, u32[]{:S(2)}, u32[]{:S(2)}) collective-permute-start(f32[2,4,5,128,2]{3,1,4,2,0:T(4,128)} %copy.90), channel_id=1, source_target_pairs={{1,0},{2,1},{3,2},{4,3},{5,4},{6,5},{7,6},{8,7},{9,8},{10,9},{11,1... | collective-permute-start | bytes 122888 | tf_op jit(solution)/shard_map/ppermute | solution.py:35
  251.1 12.3 %copy-start.4 = (f32[2,4,5,128,128]{4,2,3,1,0:T(8,128)S(1)}, f32[2,4,5,128,128]{4,2,3,1,0:T(8,128)}, u32[]{:S(2)}) copy-start(f32[2,4,5,128,128]{4,2,3,1,0:T(8,128)} %copy-done.3) | copy-start | bytes 7864324
  251.1 12.3 %copy-start.14 = (f32[5]{0:T(128)S(1)}, f32[5]{0:T(128)}, u32[]{:S(2)}) copy-start(f32[5]{0:T(128)} %copy-done.12) | copy-start | bytes 64
Sparse Core Ops, SparseCore 0:
  26.4 82.7 all-reduce.2
where the time goes:
time: 335 us; the launch traced here: 329 us
  local copies, waits for them, and re-layouts  83.6 us (25%)
  matrix products  71 us (21%)
  waiting for transfers between devices  66 us (20%)
  other arithmetic  47.7 us (14%)
  blocking collectives  30.9 us (9%)
  between operations  16.7 us (5%)
  starting transfers between devices  12.8 us (4%)
    dot_general x3, matrix products, update(): jnp.einsum('fe,gafrc->gaerc', flux_matrix, diff, precision=lax.Precision....  71 us
    psum x1, waiting for transfers between devices, broadcast(): return lax.psum(block, axis)  65.9 us
    mul x4, other arithmetic, update(): 0.5 * is_velocity * inner  36.9 us
    psum x1, blocking collectives, on_device(): sens = lax.psum(sens, 'blk')  30.9 us
    slice x6, local copies, waits for them, and re-layouts, padded_2(): leading = lax.slice_in_dim(shard, 0, width, axis=dim)  23.1 us
    gather x3, local copies, waits for them, and re-layouts, on_device(): linked = jnp.take(center, inverse, axis=3)  11.8 us
    ppermute x3, starting transfers between devices, padded_2(): before = lax.ppermute(last, axis, up)  11.7 us
    ppermute x3, local copies, waits for them, and re-layouts, padded_2(): before = lax.ppermute(last, axis, up)  9.96 us
  transfers between devices with their start and end apart: 7, of which 1 were waited for; matrix products, arithmetic and copies ran while one was open for 16% of the time, Pallas kernels for 0%

commit v1 on v0

v1 whole, which is shorter than its diff:
```python
import functools
import math

import jax
import jax.numpy as jnp
import numpy as np
from jax import lax
from jax.experimental import pallas as pl
from jax.experimental.pallas import tpu as pltpu
from jax.sharding import PartitionSpec as P

FIELDS = 5
BLADES = 96
AMP = 4
GRP_DEV = 2
STEPS = 3
R = 128
CW = 128
TILES = 16
NC = TILES * CW
N_OUT = 8
SOL = GRP_DEV * AMP
CH = CW // N_OUT
HB = 16
HF = 8
EXT = CW + 2 * HF

time_step = 0.25
second_diff = 0.1
fourth_diff = 0.02
link_weight = 0.5

UNIT = 1.0 / (time_step * link_weight)
C0 = UNIT * (1.0 - time_step * (2.0 * second_diff + 6.0 * fourth_diff + link_weight))
C1 = UNIT * time_step * (second_diff + 4.0 * fourth_diff)
C2 = -UNIT * time_step * fourth_diff

MESH = pl.DeviceIdType.MESH
F32 = jnp.float32
DIAG = (0, 2, 3, 4)


def harmonics():
    c = np.arange(-HF, CW + HF)
    phase = ((c * BLADES) % NC) / NC
    rows = [
        (np.cos if a % 2 == 0 else np.sin)(2.0 * math.pi * (a // 2 + 1) * phase) for a in range(AMP)
    ]
    table = np.zeros((EXT, 128), np.float32)
    table[:, :AMP] = np.stack(rows, axis=1)
    return table


def kernel(
    owner_s, flux_s, group_hbm, harm_hbm, link_hbm, ckpt_hbm, force_hbm,
    out_hbm, sens_ref,
    ckpt_v, force_v, group_v, harm_v, link_v, slot, picked, chosen, q, f_ext, idx, coef, pat, wf,
    mu_a, mu_b, res, sacc, sall,
    in_sem, p1_s, p1_r, p2_s, p2_r, h_s, h_r, e_s, e_r, s_s, s_r, out_sem,
):
    o = lax.axis_index("out")
    t = lax.axis_index("blk")
    up = lax.rem(t + 1, TILES)
    down = lax.rem(t + TILES - 1, TILES)

    loads = [
        pltpu.make_async_copy(src, dst, in_sem.at[i])
        for i, (src, dst) in enumerate(
            ((ckpt_hbm, ckpt_v), (force_hbm, force_v), (link_hbm, link_v.at[1]), (group_hbm, group_v), (harm_hbm, harm_v))
        )
    ]
    for c in loads:
        c.start()

    barrier = pltpu.get_barrier_semaphore()
    count = 0
    for k in range(1, N_OUT):
        pl.semaphore_signal(barrier, inc=1, device_id=(lax.rem(o + k, N_OUT), t), device_id_type=MESH)
        count += 1
    for side in (up, down):
        for k in range(N_OUT):
            pl.semaphore_signal(barrier, inc=1, device_id=(lax.rem(o + k, N_OUT), side), device_id_type=MESH)
            count += 1
    for k in range(2, TILES - 1):
        pl.semaphore_signal(barrier, inc=1, device_id=(o, lax.rem(t + k, TILES)), device_id_type=MESH)
        count += 1

    def remote(src, dst, send, recv, device):
        return pltpu.make_async_remote_copy(
            src_ref=src, dst_ref=dst, send_sem=send, recv_sem=recv, device_id=device, device_id_type=MESH
        )

    loads[0].wait()
    for f in range(FIELDS):
        slot[f] = ckpt_v[f].astype(F32).T.astype(jnp.bfloat16)
    loads[1].wait()
    for f in range(FIELDS):
        f_ext[f, HF : HF + CW, :] = force_v[f].T
    loads[2].wait()

    pl.semaphore_wait(barrier, count)

    gather = []
    for k in range(1, N_OUT):
        to = lax.rem(o + k, N_OUT)
        gather.append(
            remote(slot.at[:, pl.ds(pl.multiple_of(to * CH, CH), CH), :], picked.at[o], p1_s.at[k], p1_r.at[k], (to, t))
        )
        gather[-1].start()
    edges = [
        remote(f_ext.at[:, pl.ds(CW, HF), :], f_ext.at[:, pl.ds(0, HF), :], e_s.at[0], e_r.at[0], (o, up)),
        remote(f_ext.at[:, pl.ds(HF, HF), :], f_ext.at[:, pl.ds(HF + CW, HF), :], e_s.at[1], e_r.at[1], (o, down)),
        remote(link_v.at[1], link_v.at[0], e_s.at[2], e_r.at[2], (o, up)),
        remote(link_v.at[1], link_v.at[2], e_s.at[3], e_r.at[3], (o, down)),
    ]
    for c in edges:
        c.start()
    mine = pl.ds(pl.multiple_of(o * CH, CH), CH)
    for f in range(FIELDS):
        picked[o, f] = slot[f, mine, :]

    loads[3].wait()
    loads[4].wait()
    lane = lax.broadcasted_iota(jnp.int32, (EXT, 128), 1)
    col = lax.broadcasted_iota(jnp.int32, (EXT, 128), 0) - HF
    column = lax.rem(t * CW + col + NC, NC)
    blade = lax.shift_right_logical(column * BLADES, 11)
    group_of = jnp.sum(jnp.where(blade == lane, jnp.broadcast_to(group_v[...], (EXT, 128)), 0), axis=1, keepdims=True)
    for a in range(AMP):
        wave = harm_v[:, a : a + 1]
        for g in range(GRP_DEV):
            pat[g * AMP + a] = jnp.broadcast_to(jnp.where(group_of == o * GRP_DEV + g, wave, 0.0), (EXT, 128))
    weight = 1.0 + 2.0 * column[HF : HF + CW].astype(F32) / NC
    wf[...] = jnp.zeros_like(wf)
    for f in range(FIELDS):
        wf[f, HF : HF + CW, :] = f_ext[f, HF : HF + CW, :] * weight
    sacc[...] = jnp.zeros_like(sacc)

    for k in range(1, N_OUT):
        gather[k - 1].wait_recv()
    spread = []
    here = pl.ds(pl.multiple_of(HB + o * CH, CH), CH)
    for i, n in enumerate(reversed(range(STEPS))):
        for f in range(FIELDS):
            piece = picked[owner_s[n], f]
            chosen[i, f] = piece
            q[i, f, here, :] = piece
    for i in range(STEPS):
        for k in range(1, N_OUT):
            to = lax.rem(o + k, N_OUT)
            spread.append(remote(chosen.at[i], q.at[i, :, here, :], p2_s.at[i, k], p2_r.at[i, k], (to, t)))
            spread[-1].start()

        @pl.when(o == 0)
        def _():
            for k in range(N_OUT):
                remote(chosen.at[i], q.at[i, :, pl.ds(HB + CW, HB), :], h_s.at[i, k], h_r.at[i, 1], (k, down)).start()

        @pl.when(o == N_OUT - 1)
        def _():
            for k in range(N_OUT):
                remote(chosen.at[i], q.at[i, :, pl.ds(0, HB), :], h_s.at[i, k], h_r.at[i, 0], (k, up)).start()

    for c in edges:
        c.wait_recv()
    sub = lax.broadcasted_iota(jnp.int32, (R, 128), 0)
    lan = lax.broadcasted_iota(jnp.int32, (R, 128), 1)
    for side, (lo, n) in enumerate(((0, HF), (HF, CW), (HF + CW, HF))):
        links = jnp.broadcast_to(link_v[side], (R, 128)).T
        inverse = jnp.sum(jnp.where(links == lan, sub, 0), axis=0, keepdims=True)
        idx[lo : lo + n, :] = jnp.broadcast_to(inverse, (n, 128))

    for s in range(SOL):
        for f in range(FIELDS):
            mu_a[s, f] = f_ext[f] * pat[s]
            for lo in (0, HF + CW):
                mu_b[s, f, lo : lo + HF, :] = jnp.zeros((HF, R), F32)

    def state(i):
        for k in range(1, N_OUT):
            spread[i * (N_OUT - 1) + k - 1].wait_recv()
        for side, rows in enumerate((pl.ds(0, HB), pl.ds(HB + CW, HB))):
            remote(chosen.at[i], q.at[i, :, rows, :], h_s.at[i, 0], h_r.at[i, side], (o, up)).wait_recv()

        def body(b, carry):
            rows = pl.ds(pl.multiple_of(b * 16, 16), 16)
            half = [0.5 * q[i, f, rows, :].astype(F32) for f in range(FIELDS)]
            for f in range(FIELDS):
                v = half[f] + flux_s[f, 1]
                coef[f, rows, :] = v + half[1] if f == 1 else v
            for m, e in enumerate(DIAG):
                coef[FIELDS + m, rows, :] = half[1] + flux_s[e, e]
            return carry

        lax.fori_loop(0, (CW + 2 * HB) // 16, body, 0)

    def advance(mu, s, e0, perm, co):
        near = [[mu[s, f, pl.ds(e0 + k, 8), :] for k in (-2, -1, 0, 1, 2)] for f in range(FIELDS)]
        d = [near[f][3] - near[f][1] for f in range(FIELDS)]
        new = []
        for e in range(FIELDS):
            m2, m1, m0, p1, p2 = near[e]
            v = C0 * m0 + C1 * (m1 + p1) + C2 * (m2 + p2) + jnp.take_along_axis(m0, perm, axis=1, mode="promise_in_bounds")
            for f in range(FIELDS):
                if e == 1:
                    v = v + co[f] * d[f]
                elif e == f:
                    v = v + co[FIELDS + DIAG.index(e)] * d[f]
                else:
                    v = v + flux_s[f, e] * d[f]
            new.append(v)
        return new

    def middle(i, src, dst):
        grown = UNIT ** (i + 1)

        def body(j, carry):
            e0 = 4 + 8 * j
            rows = pl.ds(e0, 8)
            perm = idx[rows, :]
            co = [coef[m, pl.ds(e0 + HB - HF, 8), :] for m in range(9)]
            fs = [f_ext[f, rows, :] * grown for f in range(FIELDS)]
            ws = [wf[f, rows, :] * (1.0 / grown) for f in range(FIELDS)]
            for s in range(SOL):
                new = advance(src, s, e0, perm, co)
                ps = pat[s, rows, :]
                acc = sacc[s]
                for f in range(FIELDS):
                    acc = acc + new[f] * ws[f]
                    dst[s, f, rows, :] = new[f] + fs[f] * ps
                sacc[s] = acc
            return carry

        lax.fori_loop(0, 17, body, 0)

    state(0)
    middle(0, mu_a, mu_b)
    state(1)
    middle(1, mu_b, mu_a)
    state(2)
    shrink = 1.0 / UNIT**STEPS

    def last(j, carry):
        e0 = HF + 8 * j
        rows = pl.ds(e0, 8)
        perm = idx[rows, :]
        co = [coef[m, pl.ds(e0 + HB - HF, 8), :] for m in range(9)]
        ws = [wf[f, rows, :] for f in range(FIELDS)]
        for s in range(SOL):
            new = advance(mu_a, s, e0, perm, co)
            acc = sacc[s]
            for f in range(FIELDS):
                v = new[f] * shrink
                acc = acc + v * ws[f]
                mu_b[s, f, rows, :] = v
            sacc[s] = acc
        return carry

    lax.fori_loop(0, CW // 8, last, 0)

    for s in range(SOL):
        sall[t, s : s + 1, :] = jnp.sum(sacc[s], axis=0, keepdims=True)
    terms = []
    for k in range(1, TILES):
        terms.append(remote(sall.at[t], sall.at[t], s_s.at[k], s_r.at[k], (o, lax.rem(t + k, TILES))))
        terms[-1].start()

    def flip(s, carry):
        for f in range(FIELDS):
            res[s, f] = mu_b[s, f, HF : HF + CW, :].T
        pltpu.make_async_copy(res.at[s], out_hbm.at[s], out_sem.at[s]).start()
        return carry

    lax.fori_loop(0, SOL, flip, 0)

    for c in terms:
        c.wait_recv()
    total = sall[0]
    for k in range(1, TILES):
        total = total + sall[k]
    total = jnp.sum(total, axis=1, keepdims=True) * (1.0 / math.sqrt(FIELDS * R * NC))
    row8 = lax.broadcasted_iota(jnp.int32, (SOL, 128), 0)
    lane8 = lax.broadcasted_iota(jnp.int32, (SOL, 128), 1)
    for g in range(GRP_DEV):
        line = jnp.sum(jnp.where(row8 == lane8 + g * AMP, total, 0.0), axis=0, keepdims=True)
        sens_ref[g : g + 1, :] = line[:, :AMP]

    for c in terms + edges + gather + spread:
        c.wait_send()
    for i in range(STEPS):

        @pl.when(lax.rem(o + 1, N_OUT) < 2)
        def _():
            for k in range(N_OUT):
                remote(chosen.at[i], q.at[i, :, pl.ds(0, HB), :], h_s.at[i, k], h_r.at[i, 0], (k, up)).wait_send()

    for s in range(SOL):
        pltpu.make_async_copy(res.at[s], out_hbm.at[s], out_sem.at[s]).wait()


def on_device(checkpoints, owner, flux_matrix, row_link, blade_group, forcing):
    smem = pl.BlockSpec(memory_space=pltpu.SMEM)
    hbm = pl.BlockSpec(memory_space=pl.ANY)
    vmem = pl.BlockSpec(memory_space=pltpu.VMEM)
    bf16 = jnp.bfloat16
    adjoint, sens = pl.pallas_call(
        kernel,
        out_shape=(
            jax.ShapeDtypeStruct((SOL, FIELDS, R, CW), F32),
            jax.ShapeDtypeStruct((GRP_DEV, AMP), F32),
        ),
        in_specs=[smem, smem, hbm, hbm, hbm, hbm, hbm],
        out_specs=(hbm, vmem),
        scratch_shapes=[
            pltpu.VMEM((FIELDS, R, CW), bf16),
            pltpu.VMEM((FIELDS, R, CW), F32),
            pltpu.VMEM((1, 128), jnp.int32),
            pltpu.VMEM((EXT, 128), F32),
            pltpu.VMEM((3, 1, R), jnp.int32),
            pltpu.VMEM((FIELDS, CW, R), bf16),
            pltpu.VMEM((N_OUT, FIELDS, CH, R), bf16),
            pltpu.VMEM((STEPS, FIELDS, CH, R), bf16),
            pltpu.VMEM((STEPS, FIELDS, CW + 2 * HB, R), bf16),
            pltpu.VMEM((FIELDS, EXT, R), F32),
            pltpu.VMEM((EXT, R), jnp.int32),
            pltpu.VMEM((9, CW + 2 * HB, R), F32),
            pltpu.VMEM((SOL, EXT, R), F32),
            pltpu.VMEM((FIELDS, EXT, R), F32),
            pltpu.VMEM((SOL, FIELDS, EXT, R), F32),
            pltpu.VMEM((SOL, FIELDS, EXT, R), F32),
            pltpu.VMEM((SOL, FIELDS, R, CW), F32),
            pltpu.VMEM((SOL, 8, 128), F32),
            pltpu.VMEM((TILES, SOL, 128), F32),
            pltpu.SemaphoreType.DMA((5,)),
            pltpu.SemaphoreType.DMA((N_OUT,)),
            pltpu.SemaphoreType.DMA((N_OUT,)),
            pltpu.SemaphoreType.DMA((STEPS, N_OUT)),
            pltpu.SemaphoreType.DMA((STEPS, N_OUT)),
            pltpu.SemaphoreType.DMA((STEPS, N_OUT)),
            pltpu.SemaphoreType.DMA((STEPS, 2)),
            pltpu.SemaphoreType.DMA((4,)),
            pltpu.SemaphoreType.DMA((4,)),
            pltpu.SemaphoreType.DMA((TILES,)),
            pltpu.SemaphoreType.DMA((TILES,)),
            pltpu.SemaphoreType.DMA((SOL,)),
        ],
        compiler_params=pltpu.CompilerParams(collective_id=0, has_side_effects=True),
    )(
        owner,
        flux_matrix,
        jnp.pad(blade_group, (0, 128 - BLADES)).reshape(1, 128),
        jnp.asarray(harmonics()),
        row_link,
        checkpoints[0],
        forcing,
    )
    return adjoint.reshape(GRP_DEV, AMP, FIELDS, R, CW), sens


def solution(mesh):
    return jax.shard_map(
        on_device,
        mesh=mesh,
        in_specs=(P("out", None, None, "blk"), P(), P(), P("blk", None), P(), P(None, None, "blk")),
        out_specs=(P("out", None, None, None, "blk"), P("out", None)),
        check_vma=False,
    )
```

time: 335 us -> 42.4 us (0.13); the launches traced: 329 us -> 42.2 us
  local copies, waits for them, and re-layouts: 83.6 us -> 5.27 us
  matrix products: 71 us -> 0 us
  waiting for transfers between devices: 66 us -> 0 us
  other arithmetic: 47.7 us -> 0 us
  Pallas kernels: 0 us -> 36.3 us
  blocking collectives: 30.9 us -> 0 us
  between operations: 16.7 us -> 0.65 us
  starting transfers between devices: 12.8 us -> 0 us
    dot_general x3 -> x0, matrix products: 71 us -> none  [update(): jnp.einsum('fe,gafrc->gaerc', flux_matrix, diff, precision=lax.Precision....]
    psum x1 -> x0, waiting for transfers between devices: 65.9 us -> none  [broadcast(): return lax.psum(block, axis)]
    mul x14 -> x0, other arithmetic: 40.7 us -> none  [the longest x4 36.9 us: update(): 0.5 * is_velocity * inner]
    pallas_call x0 -> x1, Pallas kernels: none -> 36.3 us  [on_device(): pl.pallas_call(kernel, out_shape=(jax.ShapeDtypeStruct((SOL, FIELDS, R, C...]
    slice x10 -> x0, local copies, waits for them, and re-layouts: 32.9 us -> none  [the longest x6 23.1 us: padded_2(): leading = lax.slice_in_dim(shard, 0, width, axis=dim)]
    psum x1 -> x0, blocking collectives: 30.9 us -> none  [on_device(): sens = lax.psum(sens, 'blk')]
    ppermute x6 -> x0, local copies, waits for them, and re-layouts: 19.3 us -> none  [the longest x3 9.96 us: padded_2(): before = lax.ppermute(last, axis, up)]
    ppermute x6 -> x0, starting transfers between devices: 12.7 us -> none  [the longest x3 11.7 us: padded_2(): before = lax.ppermute(last, axis, up)]
  transfers between devices with their start and end apart: 7 -> 0, of which waited for: 1 -> 0; matrix products, arithmetic and copies ran while one was open for 16% -> 0% of each run, Pallas kernels for 0% -> 0%
where the time goes in v1:
time: 42.4 us; the launch traced here: 42.2 us
  Pallas kernels  36.3 us (86%)
  local copies, waits for them, and re-layouts  5.27 us (12%)
  between operations  0.65 us (2%)
    pallas_call x1, Pallas kernels, on_device(): pl.pallas_call(kernel, out_shape=(jax.ShapeDtypeStruct((SOL, FIELDS, R, C...  36.3 us
    unnamed x4, local copies, waits for them, and re-layouts  4.1 us
    reshape x1, local copies, waits for them, and re-layouts, on_device(): jnp.pad(blade_group, (0, 128 - BLADES)).reshape(1, 128)  1.17 us

profile of v1, /device:TPU:1, one launch (start us, length us, event | category | flops | bytes accessed | tf_op | source)
XLA Modules:
  0.0 42.2 jit_solution(17883481763305902457)
XLA Ops:
  0.6 1.2 %pad_bitcast_fusion.group_hbm = s32[1,128]{1,0:T(1,128)} fusion(s32[96]{0:T(128)} %param.11), kind=kLoop, calls=%fused_computation | loop fusion | bytes 896 | tf_op jit(solution)/shard_map/reshape | solution.py:351
  1.8 36.3 %shard_map.86 = (f32[8,5,128,128]{3,2,1,0:T(8,128)}, f32[2,4]{1,0:T(2,128)}) custom-call(s32[8]{0:T(128)} %owner_s.1, f32[5,5]{1,0:T(8,128)} %flux_s.1, s32[1,128]{1,0:T(1,128)} %pad_bitcast_fusion.group_hbm, f32[144,128]{1,0:T(8,128)} %constant.4.clone.harm_hbm, s32[1,128]{1,0:T(1,128)} %link_hbm.1, bf16[5,128,128]{2,1,0:T(8,128)(2,1)} %bitcast.5, ...), custom_call_target="tpu_custom_call" | custom-call | tf_op jit(solution)/shard_map/pallas_call | solution.py:306
  38.1 0.0 copy-start
  38.1 3.5 %copy.11 = f32[2,4,5,128,128]{4,3,2,1,0:T(8,128)} copy(f32[2,4,5,128,128]{4,3,2,1,0:T(8,128)} %bitcast.4) | data formatting | bytes 5242880
  41.6 0.0 copy-done
  41.6 0.6 %copy.12 = f32[2,4]{1,0:T(2,128)} copy(f32[2,4]{1,0:T(2,128)S(1)} %copy-done) | data formatting | bytes 64
Async XLA Ops:
  38.1 3.5 %copy-start = (f32[2,4]{1,0:T(2,128)S(1)}, f32[2,4]{1,0:T(2,128)}, u32[]{:S(2)}) copy-start(f32[2,4]{1,0:T(2,128)} %get-tuple-element.9) | copy-start | bytes 100

commit v2 on v1

v2 whole, which is shorter than its diff:
```python
import functools
import math

import jax
import jax.numpy as jnp
import numpy as np
from jax import lax
from jax.experimental import pallas as pl
from jax.experimental.pallas import tpu as pltpu
from jax.sharding import PartitionSpec as P

FIELDS = 5
BLADES = 96
AMP = 4
GRP_DEV = 2
STEPS = 3
R = 128
CW = 128
TILES = 16
NC = TILES * CW
N_OUT = 8
SOL = GRP_DEV * AMP
CH = CW // N_OUT
HQ = 4
HF = 8
EXT = CW + 2 * HF

time_step = 0.25
second_diff = 0.1
fourth_diff = 0.02
link_weight = 0.5

UNIT = 1.0 / (time_step * link_weight)
C0 = UNIT * (1.0 - time_step * (2.0 * second_diff + 6.0 * fourth_diff + link_weight))
C1 = UNIT * time_step * (second_diff + 4.0 * fourth_diff)
C2 = -UNIT * time_step * fourth_diff

MESH = pl.DeviceIdType.MESH
F32 = jnp.float32
DIAG = (0, 2, 3, 4)
UNROLL = 4


def harmonics():
    c = np.arange(-HF, CW + HF)
    phase = ((c * BLADES) % NC) / NC
    rows = [
        (np.cos if a % 2 == 0 else np.sin)(2.0 * math.pi * (a // 2 + 1) * phase) for a in range(AMP)
    ]
    table = np.zeros((EXT, 128), np.float32)
    table[:, :AMP] = np.stack(rows, axis=1)
    return table


def kernel(
    owner_hbm, flux_hbm, group_hbm, harm_hbm, link_hbm, ckpt_hbm, force_hbm,
    res, sens_ref,
    owner_s, flux_s, group_s, ckpt_v, force_v, harm_v, link_v, slot, picked, q, pack, packed, edge_q, wide, f_ext, idx, coef, pat, wf, wfull,
    mu_a, mu_b, back, sacc, sall,
    in_sem, p1_s, p1_r, p2_s, p2_r, h_s, h_r, e_s, e_r, s_s, s_r,
):
    o = lax.axis_index("out")
    t = lax.axis_index("blk")
    up = lax.rem(t + 1, TILES)
    down = lax.rem(t + TILES - 1, TILES)

    loads = [
        pltpu.make_async_copy(src, dst, in_sem.at[i])
        for i, (src, dst) in enumerate(
            ((ckpt_hbm, ckpt_v), (force_hbm, force_v), (link_hbm, link_v.at[1]), (harm_hbm, harm_v),
             (group_hbm, group_s), (owner_hbm, owner_s), (flux_hbm, flux_s))
        )
    ]
    for c in loads:
        c.start()

    barrier = pltpu.get_barrier_semaphore()
    count = 0
    for k in range(1, N_OUT):
        pl.semaphore_signal(barrier, inc=1, device_id=(lax.rem(o + k, N_OUT), t), device_id_type=MESH)
        count += 1
    for side in (up, down):
        for k in range(N_OUT):
            pl.semaphore_signal(barrier, inc=1, device_id=(lax.rem(o + k, N_OUT), side), device_id_type=MESH)
            count += 1
    for k in range(2, TILES - 1):
        pl.semaphore_signal(barrier, inc=1, device_id=(o, lax.rem(t + k, TILES)), device_id_type=MESH)
        count += 1

    def remote(src, dst, send, recv, device):
        return pltpu.make_async_remote_copy(
            src_ref=src, dst_ref=dst, send_sem=send, recv_sem=recv, device_id=device, device_id_type=MESH
        )

    pack[...] = jnp.zeros_like(pack)
    loads[0].wait()
    for f in range(FIELDS):
        turned = ckpt_v[f].astype(F32).T
        for b in range(N_OUT):
            slot[b, f] = turned[b * CH : (b + 1) * CH].astype(jnp.bfloat16)
        pack[0, HQ * f : HQ * (f + 1), :] = turned[CW - HQ :]
        pack[1, HQ * f : HQ * (f + 1), :] = turned[:HQ]
    packed[...] = pack[...].astype(jnp.bfloat16)

    pl.semaphore_wait(barrier, count)

    gather = []
    for k in range(1, N_OUT):
        to = lax.rem(o + k, N_OUT)
        gather.append(remote(slot.at[to], picked.at[o], p1_s.at[k], p1_r.at[k], (to, t)))
        gather[-1].start()
    loads[1].wait()
    for f in range(FIELDS):
        f_ext[f, HF : HF + CW, :] = force_v[f].T
    loads[2].wait()
    edges = [
        remote(f_ext.at[:, pl.ds(CW, HF), :], f_ext.at[:, pl.ds(0, HF), :], e_s.at[0], e_r.at[0], (o, up)),
        remote(f_ext.at[:, pl.ds(HF, HF), :], f_ext.at[:, pl.ds(HF + CW, HF), :], e_s.at[1], e_r.at[1], (o, down)),
        remote(link_v.at[1], link_v.at[0], e_s.at[2], e_r.at[2], (o, up)),
        remote(link_v.at[1], link_v.at[2], e_s.at[3], e_r.at[3], (o, down)),
    ]
    rims = [
        remote(packed.at[side], edge_q.at[side, o], h_s.at[side, k], h_r.at[side, k], (lax.rem(o + k, N_OUT), to))
        for side, to in enumerate((up, down))
        for k in range(N_OUT)
    ]
    for c in edges + rims:
        c.start()
    for f in range(FIELDS):
        picked[o, f] = slot[o, f]

    for c in loads[3:]:
        c.wait()
    col = lax.broadcasted_iota(jnp.int32, (EXT, 128), 0) - HF
    column = lax.rem(t * CW + col + NC, NC)
    blade = lax.shift_right_logical((col + CW) * BLADES, 11)
    group_of = jnp.zeros((EXT, 128), jnp.int32)
    per = BLADES // TILES
    for b in range(per - 1, 2 * per + 1):
        group_of = jnp.where(blade == b, group_s[lax.rem(t * per + b + BLADES - per, BLADES)], group_of)
    for a in range(AMP):
        wave = jnp.broadcast_to(harm_v[:, a : a + 1], (EXT, 128))
        for g in range(GRP_DEV):
            pat[g * AMP + a] = jnp.where(group_of == o * GRP_DEV + g, wave, 0.0)
    weight = 1.0 + 2.0 * column.astype(F32) / NC

    for c in gather:
        c.wait_recv()
    spread = []
    for i, n in enumerate(reversed(range(STEPS))):
        for f in range(FIELDS):
            q[i, o, f] = picked[owner_s[n], f]
        for k in range(1, N_OUT):
            spread.append(remote(q.at[i, o], q.at[i, o], p2_s.at[i, k], p2_r.at[i, k], (lax.rem(o + k, N_OUT), t)))
            spread[-1].start()

    for c in edges:
        c.wait_recv()
    sub = lax.broadcasted_iota(jnp.int32, (R, 128), 0)
    lan = lax.broadcasted_iota(jnp.int32, (R, 128), 1)
    for side, (lo, n) in enumerate(((0, HF), (HF, CW), (HF + CW, HF))):
        links = jnp.broadcast_to(link_v[side], (R, 128)).T
        inverse = jnp.sum(jnp.where(links == lan, sub, 0), axis=0, keepdims=True)
        idx[lo : lo + n, :] = jnp.broadcast_to(inverse, (n, 128))

    for f in range(FIELDS):
        force = f_ext[f]
        weighted = force * weight
        wfull[f] = weighted
        wf[f] = jnp.where((col >= 0) & (col < CW), weighted, 0.0)
        for s in range(SOL):
            mu_a[s, f] = force * pat[s]
    inner = wf[0, HF : HF + CW] * f_ext[0, HF : HF + CW]
    for f in range(1, FIELDS):
        inner = inner + wf[f, HF : HF + CW] * f_ext[f, HF : HF + CW]
    for s in range(SOL):
        start = (-2.0 * inner) * pat[s, HF : HF + CW]
        sacc[s] = jnp.sum(start.reshape(CW // 8, 8, 128), axis=0)
        for f in range(FIELDS):
            for lo in (0, HF + CW):
                mu_b[s, f, lo : lo + HF, :] = jnp.zeros((HF, R), F32)

    def stencil(m2, m1, m0, p1, p2, perm):
        moved = jnp.take_along_axis(m0, perm, axis=1, mode="promise_in_bounds")
        return C0 * m0 + C1 * (m1 + p1) + C2 * (m2 + p2) + moved

    def advance(mu, s, e0, perm, mix):
        near = [[mu[s, f, pl.ds(e0 + k, 8), :] for k in (-2, -1, 0, 1, 2)] for f in range(FIELDS)]
        d = [near[f][3] - near[f][1] for f in range(FIELDS)]
        new = []
        for e in range(FIELDS):
            v = stencil(*near[e], perm)
            for f in range(FIELDS):
                v = v + mix(f, e) * d[f]
            new.append(v)
        return new

    def constant(f, e):
        return flux_s[f, e]

    def mixed(co):
        def mix(f, e):
            if e == 1:
                return co[f]
            return co[FIELDS + DIAG.index(e)] if e == f else flux_s[f, e]

        return mix

    def early(j, carry):
        e0 = 4 + 8 * j
        rows = pl.ds(e0, 8)
        perm = idx[rows, :]
        fs = [f_ext[f, rows, :] * UNIT for f in range(FIELDS)]

        def some(p, carry):
            for r in range(UNROLL):
                s = p * UNROLL + r
                new = advance(mu_a, s, e0, perm, constant)
                ps = pat[s, rows, :]
                for f in range(FIELDS):
                    mu_b[s, f, rows, :] = new[f] + fs[f] * ps
            return carry

        return lax.fori_loop(0, SOL // UNROLL, some, carry)

    lax.fori_loop(0, 17, early, 0)

    def state(i, n, write):
        for k in range(1, N_OUT):
            spread[i * (N_OUT - 1) + k - 1].wait_recv()

        def body(b, carry):
            write(pl.ds(pl.multiple_of(HF + b * CH, 8), CH), [0.5 * q[i, b, f].astype(F32) for f in range(FIELDS)])
            return carry

        lax.fori_loop(0, N_OUT, body, 0)
        for side, lo in enumerate((HF - HQ, HF + CW)):
            wide[...] = edge_q[side, owner_s[n]].astype(F32)
            write(pl.ds(lo, HQ), [0.5 * wide[HQ * f : HQ * (f + 1), :] for f in range(FIELDS)])

    def halves(rows, half):
        for f in range(FIELDS):
            coef[f, rows, :] = half[f]

    def blocks(rows, half):
        for f in range(FIELDS):
            v = half[f] + flux_s[f, 1]
            coef[f, rows, :] = v + half[1] if f == 1 else v
        for m, e in enumerate(DIAG):
            coef[FIELDS + m, rows, :] = half[1] + flux_s[e, e]

    for c in rims:
        c.wait_recv()
    state(0, 2, halves)

    def finish(j, carry):
        e0 = 4 + 8 * j
        rows = pl.ds(e0, 8)
        half = [coef[f, rows, :] for f in range(FIELDS)]
        ws = [wf[f, rows, :] * (1.0 / UNIT) for f in range(FIELDS)]
        for s in range(SOL):
            d = [mu_a[s, f, pl.ds(e0 + 1, 8), :] - mu_a[s, f, pl.ds(e0 - 1, 8), :] for f in range(FIELDS)]
            dot = half[0] * d[0]
            for f in range(1, FIELDS):
                dot = dot + half[f] * d[f]
            acc = sacc[s]
            for f in range(FIELDS):
                v = mu_b[s, f, rows, :] + half[1] * d[f]
                if f == 1:
                    v = v + dot
                mu_b[s, f, rows, :] = v
                acc = acc + v * ws[f]
            sacc[s] = acc
        return carry

    lax.fori_loop(0, 17, finish, 0)

    state(1, 1, blocks)

    def second(j, carry):
        e0 = 4 + 8 * j
        rows = pl.ds(e0, 8)
        perm = idx[rows, :]
        mix = mixed([coef[m, rows, :] for m in range(9)])
        fs = [f_ext[f, rows, :] * UNIT**2 for f in range(FIELDS)]

        def some(p, carry):
            for r in range(UNROLL):
                s = p * UNROLL + r
                new = advance(mu_b, s, e0, perm, mix)
                ps = pat[s, rows, :]
                for f in range(FIELDS):
                    mu_a[s, f, rows, :] = new[f] + fs[f] * ps
            return carry

        return lax.fori_loop(0, SOL // UNROLL, some, carry)

    lax.fori_loop(0, 17, second, 0)

    state(2, 0, blocks)

    def turn(j, carry):
        rows = pl.ds(4 + 8 * j, 8)
        mix = mixed([coef[m, rows, :] for m in range(9)])
        v = [wfull[e, rows, :] for e in range(FIELDS)]
        for f in range(FIELDS):
            w = mix(f, 0) * v[0]
            for e in range(1, FIELDS):
                w = w + mix(f, e) * v[e]
            back[f, rows, :] = w
        return carry

    lax.fori_loop(0, 17, turn, 0)

    def weigh(j, carry):
        e0 = pl.multiple_of(HF + 8 * j, 8)
        rows = pl.ds(e0, 8)
        perm = jnp.broadcast_to(link_v[1], (8, 128))
        ws = []
        for f in range(FIELDS):
            near = [wfull[f, pl.ds(e0 + k, 8), :] for k in (-2, -1, 0, 1, 2)]
            v = stencil(*near, perm) + back[f, pl.ds(e0 - 1, 8), :] - back[f, pl.ds(e0 + 1, 8), :]
            ws.append(near[2] * UNIT**-2 + v * UNIT**-3)
        for s in range(SOL):
            acc = sacc[s]
            for f in range(FIELDS):
                acc = acc + mu_a[s, f, rows, :] * ws[f]
            sacc[s] = acc
        return carry

    lax.fori_loop(0, CW // 8, weigh, 0)

    for s in range(SOL):
        sall[t, s : s + 1, :] = jnp.sum(sacc[s], axis=0, keepdims=True)
    terms = []
    for k in range(1, TILES):
        terms.append(remote(sall.at[t], sall.at[t], s_s.at[k], s_r.at[k], (o, lax.rem(t + k, TILES))))
        terms[-1].start()

    def third(s, carry):
        def some(p, carry):
            for r in range(UNROLL):
                e0 = pl.multiple_of(HF + 8 * (p * UNROLL + r), 8)
                rows = pl.ds(e0, 8)
                new = advance(mu_a, s, e0, idx[rows, :], mixed([coef[m, rows, :] for m in range(9)]))
                for f in range(FIELDS):
                    res[s, f, pl.ds(pl.multiple_of(e0 - HF, 8), 8), :] = new[f] * UNIT**-3
            return carry

        lax.fori_loop(0, CW // 8 // UNROLL, some, 0)
        return carry

    lax.fori_loop(0, SOL, third, 0)

    for c in terms:
        c.wait_recv()
    total = sall[0]
    for k in range(1, TILES):
        total = total + sall[k]
    total = jnp.sum(total, axis=1, keepdims=True) * (1.0 / math.sqrt(FIELDS * R * NC))
    row8 = lax.broadcasted_iota(jnp.int32, (SOL, 128), 0)
    lane8 = lax.broadcasted_iota(jnp.int32, (SOL, 128), 1)
    for g in range(GRP_DEV):
        line = jnp.sum(jnp.where(row8 == lane8 + g * AMP, total, 0.0), axis=0, keepdims=True)
        sens_ref[g : g + 1, :] = line[:, :AMP]

    for c in terms + edges + rims + gather + spread:
        c.wait_send()


def flip(turned_ref, sens_ref, out_hbm, sens_out, res, sem):
    sens_out[...] = sens_ref[...]
    copies = [pltpu.make_async_copy(res.at[s], out_hbm.at[s], sem.at[s]) for s in range(SOL)]
    for s in range(SOL):
        for f in range(FIELDS):
            res[s, f] = turned_ref[s, f].T
        copies[s].start()
    for c in copies:
        c.wait()


def on_device(checkpoints, owner, flux_matrix, row_link, blade_group, forcing):
    hbm = pl.BlockSpec(memory_space=pltpu.HBM)
    vmem = pl.BlockSpec(memory_space=pltpu.VMEM)
    bf16 = jnp.bfloat16
    dma = pltpu.SemaphoreType.DMA
    shapes = (
        jax.ShapeDtypeStruct((SOL, FIELDS, R, CW), F32),
        jax.ShapeDtypeStruct((GRP_DEV, AMP), F32),
    )
    turned, sens = pl.pallas_call(
        kernel,
        out_shape=shapes,
        in_specs=[hbm] * 7,
        out_specs=(vmem, vmem),
        scratch_shapes=[
            pltpu.SMEM((N_OUT,), jnp.int32),
            pltpu.SMEM((FIELDS, FIELDS), F32),
            pltpu.SMEM((BLADES,), jnp.int32),
            pltpu.VMEM((FIELDS, R, CW), bf16),
            pltpu.VMEM((FIELDS, R, CW), F32),
            pltpu.VMEM((EXT, 128), F32),
            pltpu.VMEM((3, 1, R), jnp.int32),
            pltpu.VMEM((N_OUT, FIELDS, CH, R), bf16),
            pltpu.VMEM((N_OUT, FIELDS, CH, R), bf16),
            pltpu.VMEM((STEPS, N_OUT, FIELDS, CH, R), bf16),
            pltpu.VMEM((2, 32, R), F32),
            pltpu.VMEM((2, 32, R), bf16),
            pltpu.VMEM((2, N_OUT, 32, R), bf16),
            pltpu.VMEM((32, R), F32),
            pltpu.VMEM((FIELDS, EXT, R), F32),
            pltpu.VMEM((EXT, R), jnp.int32),
            pltpu.VMEM((9, EXT, R), F32),
            pltpu.VMEM((SOL, EXT, R), F32),
            pltpu.VMEM((FIELDS, EXT, R), F32),
            pltpu.VMEM((FIELDS, EXT, R), F32),
            pltpu.VMEM((SOL, FIELDS, EXT, R), F32),
            pltpu.VMEM((SOL, FIELDS, EXT, R), F32),
            pltpu.VMEM((FIELDS, EXT, R), F32),
            pltpu.VMEM((SOL, 8, 128), F32),
            pltpu.VMEM((TILES, SOL, 128), F32),
            dma((7,)),
            dma((N_OUT,)),
            dma((N_OUT,)),
            dma((STEPS, N_OUT)),
            dma((STEPS, N_OUT)),
            dma((2, N_OUT)),
            dma((2, N_OUT)),
            dma((4,)),
            dma((4,)),
            dma((TILES,)),
            dma((TILES,)),
        ],
        compiler_params=pltpu.CompilerParams(collective_id=0, has_side_effects=True, vmem_limit_bytes=24 << 20),
    )(
        *(
            pltpu.with_memory_space_constraint(x, pltpu.HBM)
            for x in (owner, flux_matrix, blade_group, jnp.asarray(harmonics()), row_link, checkpoints[0], forcing)
        )
    )
    adjoint, sens = pl.pallas_call(
        flip,
        out_shape=shapes,
        in_specs=[vmem, vmem],
        out_specs=(hbm, vmem),
        scratch_shapes=[pltpu.VMEM((SOL, FIELDS, R, CW), F32), dma((SOL,))],
        compiler_params=pltpu.CompilerParams(vmem_limit_bytes=8 << 20),
    )(turned, sens)
    return adjoint.reshape(GRP_DEV, AMP, FIELDS, R, CW), sens


def solution(mesh):
    return jax.shard_map(
        on_device,
        mesh=mesh,
        in_specs=(P("out", None, None, "blk"), P(), P(), P("blk", None), P(), P(None, None, "blk")),
        out_specs=(P("out", None, None, None, "blk"), P("out", None)),
        check_vma=False,
    )
```

time: 42.4 us -> 36.1 us (0.85)
  local copies, waits for them, and re-layouts: 5.27 us -> 0 us
  Pallas kernels: 36.3 us -> 35.3 us
    unnamed x4 -> x0, local copies, waits for them, and re-layouts: 4.1 us -> none
    reshape x1 -> x0, local copies, waits for them, and re-layouts: 1.17 us -> none  [on_device(): jnp.pad(blade_group, (0, 128 - BLADES)).reshape(1, 128)]
    pallas_call x1 -> x2, Pallas kernels: 36.3 us -> 35.3 us  [the longest x1 33 us: on_device(): pl.pallas_call(kernel, out_shape=shapes, in_specs=[hbm] * 7, out_specs=(v...]
where the time goes in v2:
time: 36.1 us; the launch traced here: 36 us
  Pallas kernels  35.3 us (98%)
  between operations  0.64 us (2%)
    pallas_call x1, Pallas kernels, on_device(): pl.pallas_call(kernel, out_shape=shapes, in_specs=[hbm] * 7, out_specs=(v...  33 us
    pallas_call x1, Pallas kernels, on_device(): pl.pallas_call(flip, out_shape=shapes, in_specs=[vmem, vmem], out_specs=(...  2.28 us

profile of v2, /device:TPU:1, one launch (start us, length us, event | category | flops | bytes accessed | tf_op | source)
XLA Modules:
  0.0 36.0 jit_solution(10050814375011381257)
XLA Ops:
  0.6 33.0 %shard_map.86 = (f32[8,5,128,128]{3,2,1,0:T(8,128)S(1)}, f32[2,4]{1,0:T(2,128)S(1)}) custom-call(s32[8]{0:T(128)} %owner_hbm.1, f32[5,5]{1,0:T(8,128)} %flux_hbm.1, s32[96]{0:T(128)} %group_hbm.1, f32[144,128]{1,0:T(8,128)} %constant.2.clone.harm_hbm, s32[1,128]{1,0:T(1,128)} %link_hbm.1, bf16[5,128,128]{2,1,0:T(8,128)(2,1)} %bitcast.2, f32[5,128,128]{2,1,0:T(8,128)} %force_hbm.1), custom_call_target="tpu_custom_call" | custom-call | tf_op jit(solution)/shard_map/pallas_call | solution.py:391
  33.7 2.3 %shard_map.87 = (f32[8,5,128,128]{3,2,1,0:T(8,128)}, f32[2,4]{1,0:T(2,128)}) custom-call(f32[8,5,128,128]{3,2,1,0:T(8,128)S(1)} %get-tuple-element.6.turned_ref, f32[2,4]{1,0:T(2,128)S(1)} %get-tuple-element.7.sens_ref), custom_call_target="tpu_custom_call" | custom-call | tf_op jit(solution)/shard_map/pallas_call | solution.py:441

commit v3 on v2

--- a/solution.py
+++ b/solution.py
@@ -21,7 +21,7 @@
 N_OUT = 8
 SOL = GRP_DEV * AMP
 CH = CW // N_OUT
-HQ = 4
+HQ = 5
 HF = 8
 EXT = CW + 2 * HF
 
@@ -38,7 +38,9 @@
 MESH = pl.DeviceIdType.MESH
 F32 = jnp.float32
 DIAG = (0, 2, 3, 4)
-UNROLL = 4
+UNROLL = 8
+PAIR = 6
+WIDE = 8
 
 
 def harmonics():
@@ -55,8 +57,8 @@
 def kernel(
     owner_hbm, flux_hbm, group_hbm, harm_hbm, link_hbm, ckpt_hbm, force_hbm,
     res, sens_ref,
-    owner_s, flux_s, group_s, ckpt_v, force_v, harm_v, link_v, slot, picked, q, pack, packed, edge_q, wide, f_ext, idx, coef, pat, wf, wfull,
-    mu_a, mu_b, back, sacc, sall,
+    owner_s, flux_s, group_s, ckpt_v, force_v, harm_v, link_v, slot, picked, q, pack, packed, edge_q, wide, f_ext, idx, idx_t, coef, halves, pat, wf, dual,
+    mu_a, mu_b, back, sall,
     in_sem, p1_s, p1_r, p2_s, p2_r, h_s, h_r, e_s, e_r, s_s, s_r,
 ):
     o = lax.axis_index("out")
@@ -147,9 +149,9 @@
     for c in gather:
         c.wait_recv()
     spread = []
-    for i, n in enumerate(reversed(range(STEPS))):
+    for i in range(STEPS):
         for f in range(FIELDS):
-            q[i, o, f] = picked[owner_s[n], f]
+            q[i, o, f] = picked[owner_s[i], f]
         for k in range(1, N_OUT):
             spread.append(remote(q.at[i, o], q.at[i, o], p2_s.at[i, k], p2_r.at[i, k], (lax.rem(o + k, N_OUT), t)))
             spread[-1].start()
@@ -162,22 +164,18 @@
         links = jnp.broadcast_to(link_v[side], (R, 128)).T
         inverse = jnp.sum(jnp.where(links == lan, sub, 0), axis=0, keepdims=True)
         idx[lo : lo + n, :] = jnp.broadcast_to(inverse, (n, 128))
+        idx_t[lo : lo + n, :] = jnp.broadcast_to(link_v[side], (n, 128))
 
     for f in range(FIELDS):
         force = f_ext[f]
-        weighted = force * weight
-        wfull[f] = weighted
-        wf[f] = jnp.where((col >= 0) & (col < CW), weighted, 0.0)
+        wf[f] = force * weight
         for s in range(SOL):
             mu_a[s, f] = force * pat[s]
-    inner = wf[0, HF : HF + CW] * f_ext[0, HF : HF + CW]
-    for f in range(1, FIELDS):
-        inner = inner + wf[f, HF : HF + CW] * f_ext[f, HF : HF + CW]
-    for s in range(SOL):
-        start = (-2.0 * inner) * pat[s, HF : HF + CW]
-        sacc[s] = jnp.sum(start.reshape(CW // 8, 8, 128), axis=0)
+    for lo in (0, HF + CW):
         for f in range(FIELDS):
-            for lo in (0, HF + CW):
+            for m in range(2):
+                dual[m, f, lo : lo + HF, :] = jnp.zeros((HF, R), F32)
+            for s in range(SOL):
                 mu_b[s, f, lo : lo + HF, :] = jnp.zeros((HF, R), F32)
 
     def stencil(m2, m1, m0, p1, p2, perm):
@@ -225,12 +223,22 @@
 
     lax.fori_loop(0, 17, early, 0)
 
-    def state(i, n, write):
+    def state(n):
         for k in range(1, N_OUT):
-            spread[i * (N_OUT - 1) + k - 1].wait_recv()
+            spread[n * (N_OUT - 1) + k - 1].wait_recv()
+
+        def write(rows, half):
+            for f in range(FIELDS):
+                v = half[f] + flux_s[f, 1]
+                coef[n, f, rows, :] = v + half[1] if f == 1 else v
+            for m, e in enumerate(DIAG):
+                coef[n, FIELDS + m, rows, :] = half[1] + flux_s[e, e]
+            if n == STEPS - 1:
+                for f in range(FIELDS):
+                    halves[f, rows, :] = half[f]
 
         def body(b, carry):
-            write(pl.ds(pl.multiple_of(HF + b * CH, 8), CH), [0.5 * q[i, b, f].astype(F32) for f in range(FIELDS)])
+            write(pl.ds(pl.multiple_of(HF + b * CH, 8), CH), [0.5 * q[n, b, f].astype(F32) for f in range(FIELDS)])
             return carry
 
         lax.fori_loop(0, N_OUT, body, 0)
@@ -238,50 +246,89 @@
             wide[...] = edge_q[side, owner_s[n]].astype(F32)
             write(pl.ds(lo, HQ), [0.5 * wide[HQ * f : HQ * (f + 1), :] for f in range(FIELDS)])
 
-    def halves(rows, half):
-        for f in range(FIELDS):
-            coef[f, rows, :] = half[f]
-
-    def blocks(rows, half):
-        for f in range(FIELDS):
-            v = half[f] + flux_s[f, 1]
-            coef[f, rows, :] = v + half[1] if f == 1 else v
-        for m, e in enumerate(DIAG):
-            coef[FIELDS + m, rows, :] = half[1] + flux_s[e, e]
-
     for c in rims:
         c.wait_recv()
-    state(0, 2, halves)
+
+    def turn(n, x):
+        def body(j, carry):
+            for r in range(PAIR):
+                rows = pl.ds(jnp.minimum(HF - HQ + 8 * (j * PAIR + r), HF + CW + HQ - 8), 8)
+                mix = mixed([coef[n, m, rows, :] for m in range(9)])
+                v = [x[e, rows, :] for e in range(FIELDS)]
+                for f in range(FIELDS):
+                    w = mix(f, 0) * v[0]
+                    for e in range(1, FIELDS):
+                        w = w + mix(f, e) * v[e]
+                    back[f, rows, :] = w
+            return carry
+
+        lax.fori_loop(0, 18 // PAIR, body, 0)
+
+    def adjoint_at(x, f, e0):
+        near = [x[f, pl.ds(e0 + k, 8), :] for k in (-2, -1, 0, 1, 2)]
+        w = back[f, pl.ds(e0 - 1, 8), :] - back[f, pl.ds(e0 + 1, 8), :]
+        return (stencil(*near, idx_t[pl.ds(e0, 8), :]) + w) * (1.0 / UNIT)
+
+    def push(n, x, to):
+        state(n)
+        turn(n, x)
+
+        def body(j, carry):
+            for r in range(PAIR):
+                e0 = jnp.minimum(4 + 8 * (j * PAIR + r), HF + CW - 4)
+                for f in range(FIELDS):
+                    to[f, pl.ds(e0, 8), :] = wf[f, pl.ds(e0, 8), :] + adjoint_at(x, f, e0)
+            return carry
+
+        lax.fori_loop(0, 18 // PAIR, body, 0)
+
+    push(0, wf, dual.at[0])
+    push(1, dual.at[0], dual.at[1])
+    state(2)
+    turn(2, dual.at[1])
+
+    def weigh(j, sums):
+        for r in range(WIDE):
+            e0 = pl.multiple_of(HF + 8 * (j * WIDE + r), 8)
+            rows = pl.ds(e0, 8)
+            p = None
+            for f in range(FIELDS):
+                v = dual[0, f, rows, :] + dual[1, f, rows, :] - 2.0 * wf[f, rows, :] + adjoint_at(dual.at[1], f, e0)
+                v = v * f_ext[f, rows, :]
+                p = v if p is None else p + v
+            sums = tuple(sums[s] + p * pat[s, rows, :] for s in range(SOL))
+        return sums
+
+    sums = lax.fori_loop(0, CW // 8 // WIDE, weigh, (jnp.zeros((8, 128), F32),) * SOL)
+
+    for s in range(SOL):
+        sall[t, s : s + 1, :] = jnp.sum(sums[s], axis=0, keepdims=True)
+    terms = []
+    for k in range(1, TILES):
+        terms.append(remote(sall.at[t], sall.at[t], s_s.at[k], s_r.at[k], (o, lax.rem(t + k, TILES))))
+        terms[-1].start()
 
     def finish(j, carry):
         e0 = 4 + 8 * j
         rows = pl.ds(e0, 8)
-        half = [coef[f, rows, :] for f in range(FIELDS)]
-        ws = [wf[f, rows, :] * (1.0 / UNIT) for f in range(FIELDS)]
+        half = [halves[f, rows, :] for f in range(FIELDS)]
         for s in range(SOL):
             d = [mu_a[s, f, pl.ds(e0 + 1, 8), :] - mu_a[s, f, pl.ds(e0 - 1, 8), :] for f in range(FIELDS)]
             dot = half[0] * d[0]
             for f in range(1, FIELDS):
                 dot = dot + half[f] * d[f]
-            acc = sacc[s]
             for f in range(FIELDS):
                 v = mu_b[s, f, rows, :] + half[1] * d[f]
-                if f == 1:
-                    v = v + dot
-                mu_b[s, f, rows, :] = v
-                acc = acc + v * ws[f]
-            sacc[s] = acc
+                mu_b[s, f, rows, :] = v + dot if f == 1 else v
         return carry
 
     lax.fori_loop(0, 17, finish, 0)
-
-    state(1, 1, blocks)
 
     def second(j, carry):
         e0 = 4 + 8 * j
         rows = pl.ds(e0, 8)
         perm = idx[rows, :]
-        mix = mixed([coef[m, rows, :] for m in range(9)])
+        mix = mixed([coef[1, m, rows, :] for m in range(9)])
         fs = [f_ext[f, rows, :] * UNIT**2 for f in range(FIELDS)]
 
         def some(p, carry):
@@ -297,52 +344,12 @@
 
     lax.fori_loop(0, 17, second, 0)
 
-    state(2, 0, blocks)
-
-    def turn(j, carry):
-        rows = pl.ds(4 + 8 * j, 8)
-        mix = mixed([coef[m, rows, :] for m in range(9)])
-        v = [wfull[e, rows, :] for e in range(FIELDS)]
-        for f in range(FIELDS):
-            w = mix(f, 0) * v[0]
-            for e in range(1, FIELDS):
-                w = w + mix(f, e) * v[e]
-            back[f, rows, :] = w
-        return carry
-
-    lax.fori_loop(0, 17, turn, 0)
-
-    def weigh(j, carry):
-        e0 = pl.multiple_of(HF + 8 * j, 8)
-        rows = pl.ds(e0, 8)
-        perm = jnp.broadcast_to(link_v[1], (8, 128))
-        ws = []
-        for f in range(FIELDS):
-            near = [wfull[f, pl.ds(e0 + k, 8), :] for k in (-2, -1, 0, 1, 2)]
-            v = stencil(*near, perm) + back[f, pl.ds(e0 - 1, 8), :] - back[f, pl.ds(e0 + 1, 8), :]
-            ws.append(near[2] * UNIT**-2 + v * UNIT**-3)
-        for s in range(SOL):
-            acc = sacc[s]
-            for f in range(FIELDS):
-                acc = acc + mu_a[s, f, rows, :] * ws[f]
-            sacc[s] = acc
-        return carry
-
-    lax.fori_loop(0, CW // 8, weigh, 0)
-
-    for s in range(SOL):
-        sall[t, s : s + 1, :] = jnp.sum(sacc[s], axis=0, keepdims=True)
-    terms = []
-    for k in range(1, TILES):
-        terms.append(remote(sall.at[t], sall.at[t], s_s.at[k], s_r.at[k], (o, lax.rem(t + k, TILES))))
-        terms[-1].start()
-
     def third(s, carry):
         def some(p, carry):
             for r in range(UNROLL):
                 e0 = pl.multiple_of(HF + 8 * (p * UNROLL + r), 8)
                 rows = pl.ds(e0, 8)
-                new = advance(mu_a, s, e0, idx[rows, :], mixed([coef[m, rows, :] for m in range(9)]))
+                new = advance(mu_a, s, e0, idx[rows, :], mixed([coef[0, m, rows, :] for m in range(9)]))
                 for f in range(FIELDS):
                     res[s, f, pl.ds(pl.multiple_of(e0 - HF, 8), 8), :] = new[f] * UNIT**-3
             return carry
@@ -410,14 +417,15 @@
             pltpu.VMEM((32, R), F32),
             pltpu.VMEM((FIELDS, EXT, R), F32),
             pltpu.VMEM((EXT, R), jnp.int32),
-            pltpu.VMEM((9, EXT, R), F32),
+            pltpu.VMEM((EXT, R), jnp.int32),
+            pltpu.VMEM((STEPS, 9, EXT, R), F32),
+            pltpu.VMEM((FIELDS, EXT, R), F32),
             pltpu.VMEM((SOL, EXT, R), F32),
             pltpu.VMEM((FIELDS, EXT, R), F32),
-            pltpu.VMEM((FIELDS, EXT, R), F32),
+            pltpu.VMEM((2, FIELDS, EXT, R), F32),
             pltpu.VMEM((SOL, FIELDS, EXT, R), F32),
             pltpu.VMEM((SOL, FIELDS, EXT, R), F32),
             pltpu.VMEM((FIELDS, EXT, R), F32),
-            pltpu.VMEM((SOL, 8, 128), F32),
             pltpu.VMEM((TILES, SOL, 128), F32),
             dma((7,)),
             dma((N_OUT,)),

time: 36.1 us -> 33.6 us (0.931)
  the two profiles are of different devices: /device:TPU:1 before, /device:TPU:0 now
where the time goes in v3:
time: 33.6 us; the launch traced here: 33.4 us
  Pallas kernels  32.8 us (98%)
  between operations  0.64 us (2%)
    pallas_call x1, Pallas kernels, on_device(): pl.pallas_call(kernel, out_shape=shapes, in_specs=[hbm] * 7, out_specs=(v...  30.5 us
    pallas_call x1, Pallas kernels, on_device(): pl.pallas_call(flip, out_shape=shapes, in_specs=[vmem, vmem], out_specs=(...  2.28 us

profile of v3, /device:TPU:0, one launch (start us, length us, event | category | flops | bytes accessed | tf_op | source)
XLA Modules:
  0.0 33.4 jit_solution(7506361765972081476)
XLA Ops:
  0.6 30.5 %shard_map.86 = (f32[8,5,128,128]{3,2,1,0:T(8,128)S(1)}, f32[2,4]{1,0:T(2,128)S(1)}) custom-call(s32[8]{0:T(128)} %owner_hbm.1, f32[5,5]{1,0:T(8,128)} %flux_hbm.1, s32[96]{0:T(128)} %group_hbm.1, f32[144,128]{1,0:T(8,128)} %constant.2.clone.harm_hbm, s32[1,128]{1,0:T(1,128)} %link_hbm.1, bf16[5,128,128]{2,1,0:T(8,128)(2,1)} %bitcast.2, f32[5,128,128]{2,1,0:T(8,128)} %force_hbm.1), custom_call_target="tpu_custom_call" | custom-call | tf_op jit(solution)/shard_map/pallas_call | solution.py:398
  31.1 2.3 %shard_map.87 = (f32[8,5,128,128]{3,2,1,0:T(8,128)}, f32[2,4]{1,0:T(2,128)}) custom-call(f32[8,5,128,128]{3,2,1,0:T(8,128)S(1)} %get-tuple-element.6.turned_ref, f32[2,4]{1,0:T(2,128)S(1)} %get-tuple-element.7.sens_ref), custom_call_target="tpu_custom_call" | custom-call | tf_op jit(solution)/shard_map/pallas_call | solution.py:449

commit v4 on v3

--- a/solution.py
+++ b/solution.py
@@ -39,6 +39,7 @@
 F32 = jnp.float32
 DIAG = (0, 2, 3, 4)
 UNROLL = 8
+ORDER = (5, 3, 7, 4, 1, 2, 6)
 PAIR = 6
 WIDE = 8
 
@@ -58,12 +59,16 @@
     owner_hbm, flux_hbm, group_hbm, harm_hbm, link_hbm, ckpt_hbm, force_hbm,
     res, sens_ref,
     owner_s, flux_s, group_s, ckpt_v, force_v, harm_v, link_v, slot, picked, q, pack, packed, edge_q, wide, f_ext, idx, idx_t, coef, halves, pat, wf, dual,
-    mu_a, mu_b, back, sall,
+    mu_a, mu_b, src, back, sall,
     in_sem, p1_s, p1_r, p2_s, p2_r, h_s, h_r, e_s, e_r, s_s, s_r,
 ):
     o = lax.axis_index("out")
     t = lax.axis_index("blk")
     up = lax.rem(t + 1, TILES)
+
+    def peer(k):
+        return lax.rem(o // 2 + k // 2, N_OUT // 2) * 2 + lax.rem(o + k, 2)
+
     down = lax.rem(t + TILES - 1, TILES)
 
     loads = [
@@ -107,8 +112,8 @@
     pl.semaphore_wait(barrier, count)
 
     gather = []
-    for k in range(1, N_OUT):
-        to = lax.rem(o + k, N_OUT)
+    for k in ORDER:
+        to = peer(k)
         gather.append(remote(slot.at[to], picked.at[o], p1_s.at[k], p1_r.at[k], (to, t)))
         gather[-1].start()
     loads[1].wait()
@@ -122,9 +127,9 @@
         remote(link_v.at[1], link_v.at[2], e_s.at[3], e_r.at[3], (o, down)),
     ]
     rims = [
-        remote(packed.at[side], edge_q.at[side, o], h_s.at[side, k], h_r.at[side, k], (lax.rem(o + k, N_OUT), to))
+        remote(packed.at[side], edge_q.at[side, o], h_s.at[side, k], h_r.at[side, k], (peer(k), to))
+        for k in ORDER + (0,)
         for side, to in enumerate((up, down))
-        for k in range(N_OUT)
     ]
     for c in edges + rims:
         c.start()
@@ -152,8 +157,8 @@
     for i in range(STEPS):
         for f in range(FIELDS):
             q[i, o, f] = picked[owner_s[i], f]
-        for k in range(1, N_OUT):
-            spread.append(remote(q.at[i, o], q.at[i, o], p2_s.at[i, k], p2_r.at[i, k], (lax.rem(o + k, N_OUT), t)))
+        for k in ORDER:
+            spread.append(remote(q.at[i, o], q.at[i, o], p2_s.at[i, k], p2_r.at[i, k], (peer(k), t)))
             spread[-1].start()
 
     for c in edges:
@@ -171,6 +176,7 @@
         wf[f] = force * weight
         for s in range(SOL):
             mu_a[s, f] = force * pat[s]
+            src[s, f] = mu_a[s, f] * UNIT**2
     for lo in (0, HF + CW):
         for f in range(FIELDS):
             for m in range(2):
@@ -329,15 +335,13 @@
         rows = pl.ds(e0, 8)
         perm = idx[rows, :]
         mix = mixed([coef[1, m, rows, :] for m in range(9)])
-        fs = [f_ext[f, rows, :] * UNIT**2 for f in range(FIELDS)]
 
         def some(p, carry):
             for r in range(UNROLL):
                 s = p * UNROLL + r
                 new = advance(mu_b, s, e0, perm, mix)
-                ps = pat[s, rows, :]
-                for f in range(FIELDS):
-                    mu_a[s, f, rows, :] = new[f] + fs[f] * ps
+                for f in range(FIELDS):
+                    mu_a[s, f, rows, :] = new[f] + src[s, f, rows, :]
             return carry
 
         return lax.fori_loop(0, SOL // UNROLL, some, carry)
@@ -351,7 +355,7 @@
                 rows = pl.ds(e0, 8)
                 new = advance(mu_a, s, e0, idx[rows, :], mixed([coef[0, m, rows, :] for m in range(9)]))
                 for f in range(FIELDS):
-                    res[s, f, pl.ds(pl.multiple_of(e0 - HF, 8), 8), :] = new[f] * UNIT**-3
+                    res[s, f, pl.ds(pl.multiple_of(e0 - HF, 8), 8), :] = new[f]
             return carry
 
         lax.fori_loop(0, CW // 8 // UNROLL, some, 0)
@@ -380,7 +384,7 @@
     copies = [pltpu.make_async_copy(res.at[s], out_hbm.at[s], sem.at[s]) for s in range(SOL)]
     for s in range(SOL):
         for f in range(FIELDS):
-            res[s, f] = turned_ref[s, f].T
+            res[s, f] = (turned_ref[s, f] * UNIT**-STEPS).T
         copies[s].start()
     for c in copies:
         c.wait()
@@ -425,6 +429,7 @@
             pltpu.VMEM((2, FIELDS, EXT, R), F32),
             pltpu.VMEM((SOL, FIELDS, EXT, R), F32),
             pltpu.VMEM((SOL, FIELDS, EXT, R), F32),
+            pltpu.VMEM((SOL, FIELDS, EXT, R), F32),
             pltpu.VMEM((FIELDS, EXT, R), F32),
             pltpu.VMEM((TILES, SOL, 128), F32),
             dma((7,)),
@@ -439,7 +444,7 @@
             dma((TILES,)),
             dma((TILES,)),
         ],
-        compiler_params=pltpu.CompilerParams(collective_id=0, has_side_effects=True, vmem_limit_bytes=24 << 20),
+        compiler_params=pltpu.CompilerParams(collective_id=0, has_side_effects=True, vmem_limit_bytes=28 << 20),
     )(
         *(
             pltpu.with_memory_space_constraint(x, pltpu.HBM)

time: 33.6 us -> 32.7 us (0.973)
  Pallas kernels: 32.8 us -> 31.9 us
    pallas_call x1, Pallas kernels: 30.5 us -> 29.6 us  [on_device(): pl.pallas_call(kernel, out_shape=shapes, in_specs=[hbm] * 7, out_specs=(v...]
where the time goes in v4:
time: 32.7 us; the launch traced here: 32.6 us
  Pallas kernels  31.9 us (98%)
  between operations  0.64 us (2%)
    pallas_call x1, Pallas kernels, on_device(): pl.pallas_call(kernel, out_shape=shapes, in_specs=[hbm] * 7, out_specs=(v...  29.6 us
    pallas_call x1, Pallas kernels, on_device(): pl.pallas_call(flip, out_shape=shapes, in_specs=[vmem, vmem], out_specs=(...  2.28 us

profile of v4, /device:TPU:0, one launch (start us, length us, event | category | flops | bytes accessed | tf_op | source)
XLA Modules:
  0.0 32.6 jit_solution(3370666748516057815)
XLA Ops:
  0.6 29.6 %shard_map.86 = (f32[8,5,128,128]{3,2,1,0:T(8,128)S(1)}, f32[2,4]{1,0:T(2,128)S(1)}) custom-call(s32[8]{0:T(128)} %owner_hbm.1, f32[5,5]{1,0:T(8,128)} %flux_hbm.1, s32[96]{0:T(128)} %group_hbm.1, f32[144,128]{1,0:T(8,128)} %constant.2.clone.harm_hbm, s32[1,128]{1,0:T(1,128)} %link_hbm.1, bf16[5,128,128]{2,1,0:T(8,128)(2,1)} %bitcast.2, f32[5,128,128]{2,1,0:T(8,128)} %force_hbm.1), custom_call_target="tpu_custom_call" | custom-call | tf_op jit(solution)/shard_map/pallas_call | solution.py:402
  30.3 2.3 %shard_map.87 = (f32[8,5,128,128]{3,2,1,0:T(8,128)}, f32[2,4]{1,0:T(2,128)}) custom-call(f32[8,5,128,128]{3,2,1,0:T(8,128)S(1)} %get-tuple-element.6.turned_ref, f32[2,4]{1,0:T(2,128)S(1)} %get-tuple-element.7.sens_ref), custom_call_target="tpu_custom_call" | custom-call | tf_op jit(solution)/shard_map/pallas_call | solution.py:454

commit v5 on v4

--- a/solution.py
+++ b/solution.py
@@ -83,12 +83,12 @@
 
     barrier = pltpu.get_barrier_semaphore()
     count = 0
-    for k in range(1, N_OUT):
-        pl.semaphore_signal(barrier, inc=1, device_id=(lax.rem(o + k, N_OUT), t), device_id_type=MESH)
+    for k in ORDER:
+        pl.semaphore_signal(barrier, inc=1, device_id=(peer(k), t), device_id_type=MESH)
         count += 1
     for side in (up, down):
-        for k in range(N_OUT):
-            pl.semaphore_signal(barrier, inc=1, device_id=(lax.rem(o + k, N_OUT), side), device_id_type=MESH)
+        for k in ORDER + (0,):
+            pl.semaphore_signal(barrier, inc=1, device_id=(peer(k), side), device_id_type=MESH)
             count += 1
     for k in range(2, TILES - 1):
         pl.semaphore_signal(barrier, inc=1, device_id=(o, lax.rem(t + k, TILES)), device_id_type=MESH)

time: 32.7 us -> 32.7 us (level)
  no operation moved by 1% of the time
where the time goes in v5:
time: 32.7 us; the launch traced here: 32.6 us
  Pallas kernels  31.9 us (98%)
  between operations  0.64 us (2%)
    pallas_call x1, Pallas kernels, on_device(): pl.pallas_call(kernel, out_shape=shapes, in_specs=[hbm] * 7, out_specs=(v...  29.6 us
    pallas_call x1, Pallas kernels, on_device(): pl.pallas_call(flip, out_shape=shapes, in_specs=[vmem, vmem], out_specs=(...  2.28 us

profile of v5, /device:TPU:0, one launch (start us, length us, event | category | flops | bytes accessed | tf_op | source)
XLA Modules:
  0.0 32.6 jit_solution(8816556695124363039)
XLA Ops:
  0.6 29.6 %shard_map.86 = (f32[8,5,128,128]{3,2,1,0:T(8,128)S(1)}, f32[2,4]{1,0:T(2,128)S(1)}) custom-call(s32[8]{0:T(128)} %owner_hbm.1, f32[5,5]{1,0:T(8,128)} %flux_hbm.1, s32[96]{0:T(128)} %group_hbm.1, f32[144,128]{1,0:T(8,128)} %constant.2.clone.harm_hbm, s32[1,128]{1,0:T(1,128)} %link_hbm.1, bf16[5,128,128]{2,1,0:T(8,128)(2,1)} %bitcast.2, f32[5,128,128]{2,1,0:T(8,128)} %force_hbm.1), custom_call_target="tpu_custom_call" | custom-call | tf_op jit(solution)/shard_map/pallas_call | solution.py:402
  30.3 2.3 %shard_map.87 = (f32[8,5,128,128]{3,2,1,0:T(8,128)}, f32[2,4]{1,0:T(2,128)}) custom-call(f32[8,5,128,128]{3,2,1,0:T(8,128)S(1)} %get-tuple-element.6.turned_ref, f32[2,4]{1,0:T(2,128)S(1)} %get-tuple-element.7.sens_ref), custom_call_target="tpu_custom_call" | custom-call | tf_op jit(solution)/shard_map/pallas_call | solution.py:454
